TPU v7x, 512 devices: a whole 4x8x8 slice. The times are simulated.
512 devices in a mesh: row: 16 (over x, z_hi), col: 32 (over z_lo, y, core).
Axes of the slice: x: 4, y: 8, z: 8 (z_hi: 4, z_lo: 2; z = z_hi * 2 + z_lo), core: 2. Of those that a mesh axis runs over, the one named last changes fastest.
Arguments:
- bin_features: bfloat16 [4096, 512], P('row'), may hold values from -6 to 6
- w_left: bfloat16 [512, 32], replicated, may hold values from -0.25 to 0.25
- w_right: bfloat16 [512, 32], replicated, may hold values from -0.25 to 0.25
- depth_kernel: float32 [9, 32], replicated, may hold values from -2 to 2
- w_point: bfloat16 [32, 32], replicated, may hold values from -1 to 1
- w_head: bfloat16 [32, 24], replicated, may hold values from -1 to 1
- cotangent: bfloat16 [24, 4096, 4096], P(None, 'row', 'col'), may hold values from -6 to 6
Outputs:
- grad_features: bfloat16 [4096, 512], P('row')
- grad_w_left: float32 [512, 32], replicated
- grad_w_right: float32 [512, 32], replicated
- grad_kernel: float32 [9, 32], replicated
- grad_point: float32 [32, 32], replicated
- grad_head: float32 [32, 24], replicated
All inputs are finite; a program needn't handle non-finite values.
Results may differ from a plain program's by a relative error of at most 0.019.
Values may be sent and summed in bfloat16 or wider, within the bound.
No kernel may reach another device: no remote copies, remote signals or barrier semaphores. Data moves between devices by JAX's collectives and lax.ppermute only.
A program may use at most 64 MiB of HBM per device.

v0:
```python
import math
import jax
import jax.numpy as jnp
from jax import lax
from jax.sharding import PartitionSpec as P

DILATION_STEP = 4


def from_root(block, axis, source):
    block = jnp.where(lax.axis_index(axis) == source, block, jnp.zeros_like(block))
    return lax.psum(block, axis)


def extended(x, sides, width):
    for axis, dim in sides:
        count, length = (lax.axis_size(axis), x.shape[dim])
        up = [(i, (i + 1) % count) for i in range(count - 1)]
        down = [(j, i) for i, j in up]
        last = lax.slice_in_dim(x, length - width, length, axis=dim)
        first = lax.slice_in_dim(x, 0, width, axis=dim)
        before = lax.ppermute(last, axis, up)
        after = lax.ppermute(first, axis, down)
        x = jnp.concatenate([before, x, after], axis=dim)
    return x


def silu_slope(values):
    logistic = jax.nn.sigmoid(values)
    return logistic * (1.0 + values * (1.0 - logistic))


def depthwise(kernel_taps, padded, output_rows, output_columns):
    result = jnp.zeros((padded.shape[0], output_rows, output_columns), jnp.float32)
    for kernel_tap_row in range(3):
        for kernel_tap_column in range(3):
            result = result + kernel_taps[3 * kernel_tap_row + kernel_tap_column][
                :, None, None
            ] * padded[
                :,
                DILATION_STEP * kernel_tap_row : DILATION_STEP * kernel_tap_row + output_rows,
                DILATION_STEP * kernel_tap_column : DILATION_STEP * kernel_tap_column
                + output_columns,
            ].astype(
                jnp.float32
            )
    return result


def body(bin_features, w_left, w_right, depth_kernel, w_point, w_head, cotangent):
    rows_per_tile = bin_features.shape[0]
    columns_per_tile = cotangent.shape[2]
    chans = w_left.shape[1]
    row_count = lax.axis_size("row")
    col_count = lax.axis_size("col")
    panel_ratio = col_count // row_count
    contact_map_bins = rows_per_tile * row_count
    grad_scale = 1.0 / math.sqrt(contact_map_bins)
    row_index = lax.axis_index("row")
    col_index = lax.axis_index("col")
    left_panel = jnp.dot(bin_features, w_left, preferred_element_type=jnp.float32).astype(
        jnp.bfloat16
    )
    offset = col_index % panel_ratio * columns_per_tile
    own_rows = lax.dynamic_slice_in_dim(bin_features, offset, columns_per_tile, 0)
    right_own = jnp.dot(own_rows, w_right, preferred_element_type=jnp.float32).astype(jnp.bfloat16)
    right_panel = from_root(right_own, "row", col_index // panel_ratio)
    pair_matrix = (
        left_panel.astype(jnp.float32).T[:, :, None] + right_panel.astype(jnp.float32).T[:, None, :]
    ).astype(jnp.bfloat16)
    extended_pair = extended(pair_matrix, (("row", 1), ("col", 2)), DILATION_STEP)
    convolved_map = depthwise(depth_kernel, extended_pair, rows_per_tile, columns_per_tile)
    trunk_gradient = (
        grad_scale
        * jnp.einsum("ch,hij->cij", w_head, cotangent, preferred_element_type=jnp.float32)
    ).astype(jnp.bfloat16)
    grad_hidden = jnp.einsum(
        "co,oij->cij", w_point, trunk_gradient, preferred_element_type=jnp.float32
    )
    convolved_gradient = (grad_hidden * silu_slope(convolved_map)).astype(jnp.bfloat16)
    extended_gradient = extended(convolved_gradient, (("row", 1), ("col", 2)), DILATION_STEP)
    hidden_state = jax.nn.silu(convolved_map).astype(jnp.bfloat16)
    mixed_out = jnp.einsum("co,cij->oij", w_point, hidden_state, preferred_element_type=jnp.float32)
    centre_offset = extended_pair[
        :,
        DILATION_STEP : DILATION_STEP + rows_per_tile,
        DILATION_STEP : DILATION_STEP + columns_per_tile,
    ]
    trunk_matrix = (centre_offset.astype(jnp.float32) + mixed_out).astype(jnp.bfloat16)
    conv_f32 = convolved_gradient.astype(jnp.float32)
    backward_pass = jnp.zeros((chans, rows_per_tile, columns_per_tile), jnp.float32)
    kern_terms = []
    for kernel_tap_row in range(3):
        for kernel_tap_column in range(3):
            backward_pass = backward_pass + depth_kernel[3 * kernel_tap_row + kernel_tap_column][
                :, None, None
            ] * extended_gradient[
                :,
                DILATION_STEP * (2 - kernel_tap_row) : DILATION_STEP * (2 - kernel_tap_row)
                + rows_per_tile,
                DILATION_STEP * (2 - kernel_tap_column) : DILATION_STEP * (2 - kernel_tap_column)
                + columns_per_tile,
            ].astype(
                jnp.float32
            )
            shifted_window = extended_pair[
                :,
                DILATION_STEP * kernel_tap_row : DILATION_STEP * kernel_tap_row + rows_per_tile,
                DILATION_STEP * kernel_tap_column : DILATION_STEP * kernel_tap_column
                + columns_per_tile,
            ].astype(jnp.float32)
            kern_terms.append(jnp.sum(conv_f32 * shifted_window, axis=(1, 2)))
    kernel_part = jnp.stack(kern_terms)
    pair_gradient = trunk_gradient.astype(jnp.float32) + backward_pass
    left_part = jnp.sum(pair_gradient, axis=2).T
    right_part = jnp.sum(pair_gradient, axis=1).T
    point_part = jnp.einsum(
        "fsk,gsk->fg", hidden_state, trunk_gradient, preferred_element_type=jnp.float32
    )
    head_part = jnp.einsum(
        "ydq,gdq->yg", trunk_matrix, cotangent, preferred_element_type=jnp.float32
    )
    grad_left = lax.psum(left_part, "col").astype(jnp.bfloat16)
    column_total = lax.psum(right_part, "row").astype(jnp.bfloat16)
    all_panels = lax.all_gather(column_total, "col", axis=0, tiled=True)
    grad_right = lax.dynamic_slice_in_dim(all_panels, row_index * rows_per_tile, rows_per_tile, 0)
    grad_features = (
        jnp.dot(grad_left, w_left.T, preferred_element_type=jnp.float32)
        + jnp.dot(grad_right, w_right.T, preferred_element_type=jnp.float32)
    ).astype(jnp.bfloat16)
    contract = (((0,), (0,)), ((), ()))
    wleft_part = lax.dot_general(
        bin_features, grad_left, contract, preferred_element_type=jnp.float32
    )
    wright_part = lax.dot_general(
        bin_features, grad_right, contract, preferred_element_type=jnp.float32
    )
    kernel_sum, point_sum, head_sum = lax.psum((kernel_part, point_part, head_part), ("row", "col"))
    wleft_sum, wright_sum = lax.psum((wleft_part, wright_part), "row")
    return (
        grad_features,
        grad_scale * wleft_sum,
        grad_scale * wright_sum,
        grad_scale * kernel_sum,
        grad_scale * point_sum,
        grad_scale * head_sum,
    )


def solution(mesh):
    placed = (P("row", None), P(), P(), P(), P(), P(), P(None, "row", "col"))
    return jax.shard_map(
        body,
        mesh=mesh,
        in_specs=placed,
        out_specs=(P("row", None), P(), P(), P(), P(), P()),
        check_vma=False,
    )
```

profile of v0, /device:TPU:8, one launch (start us, length us, event | category | flops | bytes accessed | tf_op | source)
XLA Modules:
  0.0 674.3 jit_solution(18254187634809960480)
XLA Ops:
  8.4 50.8 %psum.56 = bf16[32,128]{1,0:T(8,128)(2,1)S(1)} all-reduce(bf16[32,128]{1,0:T(8,128)(2,1)S(1)} %fusion.34), channel_id=1, replica_groups=mesh['row'=16,'col'=32] {'row'}, use_global_device_ids=true, to_apply=%region_0.1 | all-reduce | flops 4096 | bytes 16384 | tf_op jit(solution)/shard_map/psum | solution.py:12
  64.8 3.5 multiply_convert_fusion.1
  68.3 1.9 collective-permute-done.1
  70.5 2.9 fusion.51
  73.5 3.6 copy.20
  77.1 3.6 copy.22
  80.8 1.9 collective-permute-start.3
  82.7 2.6 collective-permute-start.2
  85.3 3.3 collective-permute-done.2
  88.6 3.0 copy.21
  91.6 3.0 copy.23
  94.7 7.2 %maximum_maximum_fusion = (bf16[32,264,132]{2,0,1:T(8,128)(2,1)S(1)}, bf16[32,264,132]{2,0,1:T(8,128)(2,1)S(1)}) fusion(bf16[32,4,128]{2,0,1:T(8,128)(2,1)S(1)} %collective-permute-done.1, bf16[32,256,128]{2,0,1:T(8,128)(2,1)} %copy-done.1, bf16[32,4,128]{2,0,1:T(8,128)(2,1)S(1)} %collective-permute-done, bf16[32,264,4]{2,0,1:T(8,128)(2,1)} %copy.21, ...), kind=kLoop, calls=%fused_computation.20 | loop fusion | flops 17842176 | bytes 6758400 | tf_op jit(solution)/shard_map/concatenate | solution.py:24
  101.9 10.2 %multiply_convert_fusion = (bf16[32,256,128]{2,0,1:T(8,128)(2,1)}, f32[32,256,128]{2,0,1:T(8,128)}) fusion(bf16[32,264,132]{2,0,1:T(8,128)(2,1)S(1)} %get-tuple-element.34, f32[32]{0:T(128)S(1)} %get-tuple-element.48, bf16[32,4,128]{2,0,1:T(8,128)(2,1)S(1)} %collective-permute-done.1, bf16[32,256,128]{2,0,1:T(8,128)(2,1)S(1)} %copy-done.2, ...), kind=kLoop, calls=%fused_computation.50 | loop fusion | flops 36700160 | bytes 21087360 | tf_op jit(solution)/shard_map/convert_element_type | solution.py:82
  112.1 3.4 fusion.30
  115.6 3.0 convolution_bitcast_fusion.2
  119.0 13.2 %fusion.23 = (f32[32]{0:T(128)S(1)}, f32[32]{0:T(128)S(1)}, f32[32]{0:T(128)S(1)}, f32[32]{0:T(128)S(1)}, f32[32]{0:T(128)S(1)}, /*index=5*/f32[32]{0:T(128)S(1)...) fusion(bf16[32,264,132]{2,0,1:T(8,128)(2,1)} %copy-done.5, ...), kind=kOutput, calls=%fused_computation.47 | convolution fusion | flops 110100192 | bytes 23186560 | tf_op jit(solution)/shard_map/co,oij->cij/dot_general | solution.py:77
  132.3 96.0 %all-reduce = (f32[9,32]{1,0:T(8,128)S(1)}, f32[32,32]{1,0:T(8,128)S(1)}, f32[32,24]{0,1:T(8,128)S(1)}) all-reduce(f32[9,32]{1,0:T(8,128)S(1)} %stack.39, f32[32,32]{1,0:T(8,128)S(1)} %convolution_bitcast_fusion.2, f32[32,24]{0,1:T(8,128)S(1)} %fusion.30), channel_id=1, replica_groups=mesh['row'=16,'col'=32] {'row','col'}, use_global_device_ids=true, to_apply=%region_16.17 | all-reduce | flops 2080 | bytes 16640 | tf_op jit(solution)/shard_map/psum | solution.py:138
  229.7 2.8 collective-permute-start.4
  234.6 5.1 collective-permute-done.5
  241.5 2.9 fusion.50
  244.5 3.6 copy.24
  248.1 3.6 copy.26
  251.8 1.9 collective-permute-start.7
  253.7 3.6 collective-permute-start.6
  259.5 3.0 copy.25
  262.6 3.0 copy.27
  265.6 7.2 %pad_maximum_fusion.1 = (bf16[32,264,132]{2,0,1:T(8,128)(2,1)S(1)}, bf16[32,264,132]{2,0,1:T(8,128)(2,1)S(1)}) fusion(bf16[32,264,4]{2,0,1:T(8,128)(2,1)} %copy.25, bf16[32,4,128]{2,0,1:T(8,128)(2,1)S(1)} %collective-permute-done.5, bf16[32,256,128]{2,0,1:T(8,128)(2,1)} %get-tuple-element.50, bf16[32,4,128]{2,0,1:T(8,128)(2,1)S(1)} %collective-permute-done.4, ...), kind=kLoop, calls=%fused_computation.22 | loop fusion | flops 17842176 | bytes 6758400 | tf_op jit(solution)/shard_map/concatenate | solution.py:24
  272.9 7.2 %fusion.48 = (f32[32,128]{1,0:T(8,128)S(1)}, f32[32,256]{0,1:T(8,128)S(1)}) fusion(bf16[32,264,132]{2,0,1:T(8,128)(2,1)S(1)} %get-tuple-element.30, f32[32]{0:T(128)S(1)} %get-tuple-element.48, bf16[32,256,128]{2,0,1:T(8,128)(2,1)S(1)} %copy-done.6, bf16[32,4,128]{2,0,1:T(8,128)(2,1)S(1)} %collective-permute-done.4, f32[32]{0:T(128)S(1)} %get-tuple-element.49, ...), kind=kLoop, calls=%fused_computation.100 | loop fusion | flops 33542144 | bytes 16893056 | tf_op jit(solution)/shard_map/reduce_sum | solution.py:116
  280.2 102.3 %psum.57 = bf16[256,32]{1,0:T(8,128)(2,1)S(1)} all-reduce(f32[256,32]{1,0:T(8,128)S(1)} %bitcast.73), channel_id=1, replica_groups=mesh['row'=16,'col'=32] {'col'}, use_global_device_ids=true, to_apply=%region_2.3 | all-reduce | flops 8192 | bytes 49152 | tf_op jit(solution)/shard_map/psum | solution.py:123
  383.5 80.7 %psum.58 = bf16[128,32]{0,1:T(8,128)(2,1)S(1)} all-reduce(f32[128,32]{0,1:T(8,128)S(1)} %bitcast.74), channel_id=1, replica_groups=mesh['row'=16,'col'=32] {'row'}, use_global_device_ids=true, to_apply=%region_4.5 | all-reduce | flops 4096 | bytes 24576 | tf_op jit(solution)/shard_map/psum | solution.py:124
  464.2 35.4 %all_gather.3 = bf16[4096,32]{0,1:T(8,128)(2,1)S(1)} all-gather(bf16[128,32]{0,1:T(8,128)(2,1)S(1)} %psum.58), channel_id=1, replica_groups=mesh['row'=16,'col'=32] {'col'}, dimensions={0}, use_global_device_ids=true | all-gather | bytes 270336 | tf_op jit(solution)/shard_map/all_gather | solution.py:125
  501.3 164.6 %all-reduce.4.cloned.1.call-done = (f32[512,32]{0,1:T(8,128)}, f32[512,32]{0,1:T(8,128)}) async-done(((f32[512,32]{0,1:T(8,128)}, f32[512,32]{0,1:T(8,128)}), (f32[512,32]{0,1:T(8,128)}, f32[512,32]{0,1:T(8,128)})) %all-reduce.4.cloned.1.call-update) | async-done | bytes 131088 | tf_op jit(solution)/shard_map/psum | solution.py:139
  (57 shorter events, 19.4 us)
Async XLA Ops:
  7.2 57.7 %copy-start = (bf16[24,256,128]{2,1,0:T(8,128)(2,1)S(1)}, bf16[24,256,128]{2,1,0:T(8,128)(2,1)}, u32[]{:S(2)}) copy-start(bf16[24,256,128]{2,1,0:T(8,128)(2,1)} %param.13) | copy-start | bytes 4718596
  7.2 658.8 %all-reduce.4.cloned.1.call-start = ((), (), s32[]{:S(2)}) async-start(), calls=%async_computation | async-start | bytes 262144 | tf_op jit(solution)/shard_map/psum | solution.py:139
  62.2 8.0 %copy-start.1 = (bf16[32,256,128]{2,0,1:T(8,128)(2,1)}, bf16[32,256,128]{2,0,1:T(8,128)(2,1)S(1)}, u32[]{:S(2)}) copy-start(bf16[32,256,128]{2,0,1:T(8,128)(2,1)S(1)} %add_convert_fusion) | copy-start | bytes 6291460
  62.2 6.1 collective-permute-start
  63.5 6.7 collective-permute-start.1
  73.5 11.8 %copy-start.12 = (f32[9,32]{1,0:T(8,128)S(1)}, f32[9,32]{1,0:T(8,128)}, u32[]{:S(2)}) copy-start(f32[9,32]{1,0:T(8,128)} %param.10) | copy-start | bytes 3460
  80.8 10.9 %collective-permute-start.3 = (bf16[32,264,4]{1,0,2:T(8,128)(2,1)S(1)}, bf16[32,264,4]{1,0,2:T(8,128)(2,1)S(1)}, u32[]{:S(2)}, u32[]{:S(2)}) collective-permute-start(bf16[32,264,4]{1,0,2:T(8,128)(2,1)S(1)} %copy.22), channel_id=1, source_target_pairs={{1,0},{2,1},{3,2},{4,3},{5,4},{6,5},{7,6},{8,7},{9,8},{10,9},{11,1... | collective-permute-start | bytes 202760 | tf_op jit(solution)/shard_map/ppermute | solution.py:23
  82.7 5.9 collective-permute-start.2
  94.7 7.2 %copy-start.2 = (bf16[32,256,128]{2,0,1:T(8,128)(2,1)S(1)}, bf16[32,256,128]{2,0,1:T(8,128)(2,1)}, u32[]{:S(2)}) copy-start(bf16[32,256,128]{2,0,1:T(8,128)(2,1)} %copy-done.1) | copy-start | bytes 6291460
  101.9 10.2 %copy-start.4 = (bf16[32,264,132]{2,0,1:T(8,128)(2,1)}, bf16[32,264,132]{2,0,1:T(8,128)(2,1)S(1)}, u32[]{:S(2)}) copy-start(bf16[32,264,132]{2,0,1:T(8,128)(2,1)S(1)} %get-tuple-element.33) | copy-start | bytes 6690820
  101.9 10.2 %copy-start.5 = (bf16[32,264,132]{2,0,1:T(8,128)(2,1)}, bf16[32,264,132]{2,0,1:T(8,128)(2,1)S(1)}, u32[]{:S(2)}) copy-start(bf16[32,264,132]{2,0,1:T(8,128)(2,1)S(1)} %get-tuple-element.34) | copy-start | bytes 6690820
  101.9 10.2 %copy-start.13 = (bf16[32,32]{1,0:T(8,128)(2,1)S(1)}, bf16[32,32]{1,0:T(8,128)(2,1)}, u32[]{:S(2)}) copy-start(bf16[32,32]{1,0:T(8,128)(2,1)} %param.11) | copy-start | bytes 6148
  115.5 3.1 copy-start.3
  115.5 3.5 copy-start.7
  229.7 4.9 collective-permute-start.4
  232.5 7.2 %collective-permute-start.5 = (bf16[32,4,128]{2,0,1:T(8,128)(2,1)S(1)}, bf16[32,4,128]{2,0,1:T(8,128)(2,1)S(1)}, u32[]{:S(2)}, u32[]{:S(2)}) collective-permute-start(bf16[32,4,128]{2,0,1:T(8,128)(2,1)S(1)} %get-tuple-element.38), channel_id=1, source_target_pairs={{32,0},{64,32},{96,64},{128,96},{160,128},{192,160},{224,192},{256... | collective-permute-start | bytes 98312 | tf_op jit(solution)/shard_map/ppermute | solution.py:23
  251.8 10.8 %collective-permute-start.7 = (bf16[32,264,4]{1,0,2:T(8,128)(2,1)S(1)}, bf16[32,264,4]{1,0,2:T(8,128)(2,1)S(1)}, u32[]{:S(2)}, u32[]{:S(2)}) collective-permute-start(bf16[32,264,4]{1,0,2:T(8,128)(2,1)S(1)} %copy.26), channel_id=1, source_target_pairs={{0,1},{1,2},{2,3},{3,4},{4,5},{5,6},{6,7},{7,8},{8,9},{9,10},{10,1... | collective-permute-start | bytes 202760 | tf_op jit(solution)/shard_map/ppermute | solution.py:22
  253.7 5.8 collective-permute-start.6
  265.6 7.3 %copy-start.6 = (bf16[32,256,128]{2,0,1:T(8,128)(2,1)S(1)}, bf16[32,256,128]{2,0,1:T(8,128)(2,1)}, u32[]{:S(2)}) copy-start(bf16[32,256,128]{2,0,1:T(8,128)(2,1)} %get-tuple-element.50) | copy-start | bytes 6291460
  265.6 7.3 %copy-start.8 = (bf16[32,256,128]{2,0,1:T(8,128)(2,1)S(1)}, bf16[32,256,128]{2,0,1:T(8,128)(2,1)}, u32[]{:S(2)}) copy-start(bf16[32,256,128]{2,0,1:T(8,128)(2,1)} %multiply_convert_fusion.1) | copy-start | bytes 6291460
  272.9 109.6 %copy-start.9 = (bf16[256,512]{1,0:T(8,128)(2,1)S(1)}, bf16[256,512]{1,0:T(8,128)(2,1)}, u32[]{:S(2)}) copy-start(bf16[256,512]{1,0:T(8,128)(2,1)} %param.7) | copy-start | bytes 786436
  272.9 110.4 %copy-start.10 = (bf16[512,32]{0,1:T(8,128)(2,1)S(1)}, bf16[512,32]{0,1:T(8,128)(2,1)}, u32[]{:S(2)}) copy-start(bf16[512,32]{0,1:T(8,128)(2,1)} %param.8) | copy-start | bytes 98308
  272.9 227.5 %copy-start.11 = (bf16[512,32]{0,1:T(8,128)(2,1)S(1)}, bf16[512,32]{0,1:T(8,128)(2,1)}, u32[]{:S(2)}) copy-start(bf16[512,32]{0,1:T(8,128)(2,1)} %param.9) | copy-start | bytes 98308
Sparse Core Ops, SparseCore 0:
  500.5 165.3 all-reduce.3
where the time goes:
time: 675 us; the launch traced here: 674 us
  blocking collectives  365 us (54%)
  waiting for transfers between devices  176 us (26%)
  other arithmetic  39 us (6%)
  local copies, waits for them, and re-layouts  34 us (5%)
  matrix products  28.2 us (4%)
  starting transfers between devices  17 us (3%)
  between operations  14.4 us (2%)
    psum x1, waiting for transfers between devices, body(): wleft_sum, wright_sum = lax.psum((wleft_part, wright_part), 'row')  165 us
    psum x1, blocking collectives, body(): grad_left = lax.psum(left_part, 'col').astype(jnp.bfloat16)  102 us
    psum x1, blocking collectives, body(): lax.psum((kernel_part, point_part, head_part), ('row', 'col'))  96 us
    psum x1, blocking collectives, body(): column_total = lax.psum(right_part, 'row').astype(jnp.bfloat16)  80.7 us
    psum x1, blocking collectives, from_root(): return lax.psum(block, axis)  50.8 us
    all_gather x1, blocking collectives, body(): all_panels = lax.all_gather(column_total, 'col', axis=0, tiled=True)  35.4 us
    concatenate x4, other arithmetic, extended(): x = jnp.concatenate([before, x, after], axis=dim)  16.6 us
  transfers between devices with their start and end apart: 9, of which 5 were waited for; matrix products, arithmetic and copies ran while one was open for 2% of the time, Pallas kernels for 0%

commit v1 on v0

--- a/solution.py
+++ b/solution.py
@@ -122,7 +122,8 @@
     )
     grad_left = lax.psum(left_part, "col").astype(jnp.bfloat16)
     column_total = lax.psum(right_part, "row").astype(jnp.bfloat16)
-    all_panels = lax.all_gather(column_total, "col", axis=0, tiled=True)
+    sent = jnp.stack([column_total] * lax.axis_size("col"))
+    all_panels = jnp.concatenate(lax.all_to_all(sent, "col", 0, 0), axis=0)
     grad_right = lax.dynamic_slice_in_dim(all_panels, row_index * rows_per_tile, rows_per_tile, 0)
     grad_features = (
         jnp.dot(grad_left, w_left.T, preferred_element_type=jnp.float32)

time: 675 us -> 647 us (0.959)
  blocking collectives: 365 us -> 333 us
  starting transfers between devices: 17 us -> 27.1 us
    all_gather x1 -> x0, blocking collectives: 35.4 us -> none  [body(): all_panels = lax.all_gather(column_total, 'col', axis=0, tiled=True)]
    all_to_all x0 -> x1, starting transfers between devices: none -> 8.63 us  [body(): all_panels = jnp.concatenate(lax.all_to_all(sent, 'col', 0, 0), axis=0)]
  transfers between devices with their start and end apart: 9 -> 10, of which waited for: 5 -> 4; matrix products, arithmetic and copies ran while one was open for 2% -> 2% of each run, Pallas kernels for 0% -> 0%
where the time goes in v1:
time: 647 us; the launch traced here: 646 us
  blocking collectives  333 us (51%)
  waiting for transfers between devices  170 us (26%)
  other arithmetic  39 us (6%)
  local copies, waits for them, and re-layouts  35.3 us (5%)
  matrix products  27.2 us (4%)
  starting transfers between devices  27.1 us (4%)
  between operations  14.4 us (2%)
    psum x1, waiting for transfers between devices, body(): wleft_sum, wright_sum = lax.psum((wleft_part, wright_part), 'row')  163 us
    psum x1, blocking collectives, body(): grad_left = lax.psum(left_part, 'col').astype(jnp.bfloat16)  104 us
    psum x1, blocking collectives, body(): lax.psum((kernel_part, point_part, head_part), ('row', 'col'))  98.4 us
    psum x1, blocking collectives, body(): column_total = lax.psum(right_part, 'row').astype(jnp.bfloat16)  79.5 us
    psum x1, blocking collectives, from_root(): return lax.psum(block, axis)  50.8 us
    concatenate x4, other arithmetic, extended(): x = jnp.concatenate([before, x, after], axis=dim)  16.6 us
  transfers between devices with their start and end apart: 10, of which 4 were waited for; matrix products, arithmetic and copies ran while one was open for 2% of the time, Pallas kernels for 0%

profile of v1, /device:TPU:8, one launch (start us, length us, event | category | flops | bytes accessed | tf_op | source)
XLA Modules:
  0.0 645.9 jit_solution(14249898495257398312)
XLA Ops:
  8.4 50.8 %psum.56 = bf16[32,128]{1,0:T(8,128)(2,1)S(1)} all-reduce(bf16[32,128]{1,0:T(8,128)(2,1)S(1)} %fusion.34), channel_id=1, replica_groups=mesh['row'=16,'col'=32] {'row'}, use_global_device_ids=true, to_apply=%region_0.1 | all-reduce | flops 4096 | bytes 16384 | tf_op jit(solution)/shard_map/psum | solution.py:12
  64.8 3.5 multiply_convert_fusion.1
  68.3 1.9 collective-permute-done.1
  70.5 2.9 fusion.51
  73.4 3.6 copy.34
  77.1 3.6 copy.36
  80.7 1.9 collective-permute-start.3
  82.6 2.6 collective-permute-start.2
  85.3 3.3 collective-permute-done.2
  88.6 3.0 copy.35
  91.6 3.0 copy.37
  94.6 7.2 %maximum_maximum_fusion = (bf16[32,264,132]{2,0,1:T(8,128)(2,1)S(1)}, bf16[32,264,132]{2,0,1:T(8,128)(2,1)S(1)}) fusion(bf16[32,4,128]{2,0,1:T(8,128)(2,1)S(1)} %collective-permute-done.1, bf16[32,256,128]{2,0,1:T(8,128)(2,1)} %copy-done.1, bf16[32,4,128]{2,0,1:T(8,128)(2,1)S(1)} %collective-permute-done, bf16[32,264,4]{2,0,1:T(8,128)(2,1)} %copy.35, ...), kind=kLoop, calls=%fused_computation.20 | loop fusion | flops 17842176 | bytes 6758400 | tf_op jit(solution)/shard_map/concatenate | solution.py:24
  101.9 10.2 %multiply_convert_fusion = (bf16[32,256,128]{2,0,1:T(8,128)(2,1)}, f32[32,256,128]{2,0,1:T(8,128)}) fusion(bf16[32,264,132]{2,0,1:T(8,128)(2,1)S(1)} %get-tuple-element.34, f32[32]{0:T(128)S(1)} %get-tuple-element.48, bf16[32,4,128]{2,0,1:T(8,128)(2,1)S(1)} %collective-permute-done.1, bf16[32,256,128]{2,0,1:T(8,128)(2,1)S(1)} %copy-done.2, ...), kind=kLoop, calls=%fused_computation.50 | loop fusion | flops 36700160 | bytes 21087360 | tf_op jit(solution)/shard_map/convert_element_type | solution.py:82
  112.1 3.4 fusion.30
  115.5 3.0 convolution_bitcast_fusion.2
  119.0 12.2 %fusion.23 = (f32[32]{0:T(128)S(1)}, f32[32]{0:T(128)S(1)}, f32[32]{0:T(128)S(1)}, f32[32]{0:T(128)S(1)}, f32[32]{0:T(128)S(1)}, /*index=5*/f32[32]{0:T(128)S(1)...) fusion(bf16[32,264,132]{2,0,1:T(8,128)(2,1)} %copy-done.5, ...), kind=kOutput, calls=%fused_computation.47 | convolution fusion | flops 110100192 | bytes 23186560 | tf_op jit(solution)/shard_map/co,oij->cij/dot_general | solution.py:77
  132.6 4.5 collective-permute-start.4
  138.5 98.4 %all-reduce = (f32[9,32]{1,0:T(8,128)S(1)}, f32[32,32]{1,0:T(8,128)S(1)}, f32[32,24]{0,1:T(8,128)S(1)}) all-reduce(f32[9,32]{1,0:T(8,128)S(1)} %stack.32, f32[32,32]{1,0:T(8,128)S(1)} %convolution_bitcast_fusion.2, f32[32,24]{0,1:T(8,128)S(1)} %fusion.30), channel_id=1, replica_groups=mesh['row'=16,'col'=32] {'row','col'}, use_global_device_ids=true, to_apply=%region_16.17 | all-reduce | flops 2080 | bytes 16640 | tf_op jit(solution)/shard_map/psum | solution.py:139
  237.5 1.9 pad_maximum_fusion.3
  239.4 2.9 fusion.50
  242.3 3.6 copy.38
  246.0 3.6 copy.40
  249.6 1.9 collective-permute-start.7
  251.5 3.6 collective-permute-start.6
  257.4 3.0 copy.39
  260.4 3.0 copy.41
  263.4 7.2 %pad_maximum_fusion.1 = (bf16[32,264,132]{2,0,1:T(8,128)(2,1)S(1)}, bf16[32,264,132]{2,0,1:T(8,128)(2,1)S(1)}) fusion(bf16[32,264,4]{2,0,1:T(8,128)(2,1)} %copy.39, bf16[32,4,128]{2,0,1:T(8,128)(2,1)S(1)} %collective-permute-done.5, bf16[32,256,128]{2,0,1:T(8,128)(2,1)} %copy-done.6, bf16[32,4,128]{2,0,1:T(8,128)(2,1)S(1)} %collective-permute-done.4, ...), kind=kLoop, calls=%fused_computation.22 | loop fusion | flops 17842176 | bytes 6758400 | tf_op jit(solution)/shard_map/concatenate | solution.py:24
  270.7 7.2 %fusion.48 = (f32[32,128]{1,0:T(8,128)S(1)}, f32[32,256]{0,1:T(8,128)S(1)}) fusion(bf16[32,264,132]{2,0,1:T(8,128)(2,1)S(1)} %get-tuple-element.30, f32[32]{0:T(128)S(1)} %get-tuple-element.48, bf16[32,256,128]{2,0,1:T(8,128)(2,1)S(1)} %copy-done.7, bf16[32,4,128]{2,0,1:T(8,128)(2,1)S(1)} %collective-permute-done.4, f32[32]{0:T(128)S(1)} %get-tuple-element.49, ...), kind=kLoop, calls=%fused_computation.101 | loop fusion | flops 33542144 | bytes 16893056 | tf_op jit(solution)/shard_map/reduce_sum | solution.py:116
  278.0 79.5 %psum.58 = bf16[128,32]{0,1:T(8,128)(2,1)S(1)} all-reduce(f32[128,32]{0,1:T(8,128)S(1)} %bitcast.80), channel_id=1, replica_groups=mesh['row'=16,'col'=32] {'row'}, use_global_device_ids=true, to_apply=%region_4.5 | all-reduce | flops 4096 | bytes 24576 | tf_op jit(solution)/shard_map/psum | solution.py:124
  358.2 8.6 %all-to-all-start = ((bf16[32,128,32]{1,2,0:T(8,128)(2,1)}), bf16[32,128,32]{1,2,0:T(8,128)(2,1)S(1)}, u32[]{:S(2)}, u32[]{:S(2)}) async-start(bf16[32,128,32]{1,2,0:T(8,128)(2,1)} %stack.22), calls=%async_computation | async-start | bytes 524288 | tf_op jit(solution)/shard_map/all_to_all | solution.py:126
  367.5 104.4 %psum.57 = bf16[256,32]{1,0:T(8,128)(2,1)S(1)} all-reduce(f32[256,32]{1,0:T(8,128)S(1)} %bitcast.79), channel_id=1, replica_groups=mesh['row'=16,'col'=32] {'col'}, use_global_device_ids=true, to_apply=%region_2.3 | all-reduce | flops 8192 | bytes 49152 | tf_op jit(solution)/shard_map/psum | solution.py:123
  474.8 162.8 %all-reduce.4.cloned.1.call-done = (f32[512,32]{0,1:T(8,128)}, f32[512,32]{0,1:T(8,128)}) async-done(((f32[512,32]{0,1:T(8,128)}, f32[512,32]{0,1:T(8,128)}), (f32[512,32]{0,1:T(8,128)}, f32[512,32]{0,1:T(8,128)})) %all-reduce.4.cloned.1.call-update) | async-done | bytes 131088 | tf_op jit(solution)/shard_map/psum | solution.py:140
  (62 shorter events, 18.6 us)
Async XLA Ops:
  7.2 57.6 %copy-start = (bf16[24,256,128]{2,1,0:T(8,128)(2,1)S(1)}, bf16[24,256,128]{2,1,0:T(8,128)(2,1)}, u32[]{:S(2)}) copy-start(bf16[24,256,128]{2,1,0:T(8,128)(2,1)} %param.13) | copy-start | bytes 4718596
  62.2 8.0 %copy-start.1 = (bf16[32,256,128]{2,0,1:T(8,128)(2,1)}, bf16[32,256,128]{2,0,1:T(8,128)(2,1)S(1)}, u32[]{:S(2)}) copy-start(bf16[32,256,128]{2,0,1:T(8,128)(2,1)S(1)} %add_convert_fusion) | copy-start | bytes 6291460
  62.2 6.1 collective-permute-start
  63.5 6.7 %collective-permute-start.1 = (bf16[32,4,128]{2,0,1:T(8,128)(2,1)S(1)}, bf16[32,4,128]{2,0,1:T(8,128)(2,1)S(1)}, u32[]{:S(2)}, u32[]{:S(2)}) collective-permute-start(bf16[32,4,128]{2,0,1:T(8,128)(2,1)S(1)} %get-tuple-element.40), channel_id=1, source_target_pairs={{32,0},{64,32},{96,64},{128,96},{160,128},{192,160},{224,192},{256... | collective-permute-start | bytes 98312 | tf_op jit(solution)/shard_map/ppermute | solution.py:23
  73.4 11.8 %copy-start.13 = (f32[9,32]{1,0:T(8,128)S(1)}, f32[9,32]{1,0:T(8,128)}, u32[]{:S(2)}) copy-start(f32[9,32]{1,0:T(8,128)} %param.10) | copy-start | bytes 3460
  80.7 10.9 %collective-permute-start.3 = (bf16[32,264,4]{1,0,2:T(8,128)(2,1)S(1)}, bf16[32,264,4]{1,0,2:T(8,128)(2,1)S(1)}, u32[]{:S(2)}, u32[]{:S(2)}) collective-permute-start(bf16[32,264,4]{1,0,2:T(8,128)(2,1)S(1)} %copy.36), channel_id=1, source_target_pairs={{1,0},{2,1},{3,2},{4,3},{5,4},{6,5},{7,6},{8,7},{9,8},{10,9},{11,1... | collective-permute-start | bytes 202760 | tf_op jit(solution)/shard_map/ppermute | solution.py:23
  82.6 5.9 collective-permute-start.2
  94.6 7.2 %copy-start.2 = (bf16[32,256,128]{2,0,1:T(8,128)(2,1)S(1)}, bf16[32,256,128]{2,0,1:T(8,128)(2,1)}, u32[]{:S(2)}) copy-start(bf16[32,256,128]{2,0,1:T(8,128)(2,1)} %copy-done.1) | copy-start | bytes 6291460
  101.9 10.2 %copy-start.4 = (bf16[32,264,132]{2,0,1:T(8,128)(2,1)}, bf16[32,264,132]{2,0,1:T(8,128)(2,1)S(1)}, u32[]{:S(2)}) copy-start(bf16[32,264,132]{2,0,1:T(8,128)(2,1)S(1)} %get-tuple-element.33) | copy-start | bytes 6690820
  101.9 10.2 %copy-start.5 = (bf16[32,264,132]{2,0,1:T(8,128)(2,1)}, bf16[32,264,132]{2,0,1:T(8,128)(2,1)S(1)}, u32[]{:S(2)}) copy-start(bf16[32,264,132]{2,0,1:T(8,128)(2,1)S(1)} %get-tuple-element.34) | copy-start | bytes 6690820
  101.9 10.2 %copy-start.14 = (bf16[32,32]{1,0:T(8,128)(2,1)S(1)}, bf16[32,32]{1,0:T(8,128)(2,1)}, u32[]{:S(2)}) copy-start(bf16[32,32]{1,0:T(8,128)(2,1)} %param.11) | copy-start | bytes 6148
  115.5 3.1 copy-start.3
  115.5 3.5 copy-start.8
  131.2 1.3 copy-start.6
  132.6 104.9 %collective-permute-start.4 = (bf16[32,4,128]{2,0,1:T(8,128)(2,1)S(1)}, bf16[32,4,128]{2,0,1:T(8,128)(2,1)S(1)}, u32[]{:S(2)}, u32[]{:S(2)}) collective-permute-start(bf16[32,4,128]{2,0,1:T(8,128)(2,1)S(1)} %get-tuple-element.37), channel_id=1, source_target_pairs={{0,32},{32,64},{64,96},{96,128},{128,160},{160,192},{192,224},{224... | collective-permute-start | bytes 98312 | tf_op jit(solution)/shard_map/ppermute | solution.py:22
  137.1 100.4 %collective-permute-start.5 = (bf16[32,4,128]{2,0,1:T(8,128)(2,1)S(1)}, bf16[32,4,128]{2,0,1:T(8,128)(2,1)S(1)}, u32[]{:S(2)}, u32[]{:S(2)}) collective-permute-start(bf16[32,4,128]{2,0,1:T(8,128)(2,1)S(1)} %get-tuple-element.38), channel_id=1, source_target_pairs={{32,0},{64,32},{96,64},{128,96},{160,128},{192,160},{224,192},{256... | collective-permute-start | bytes 98312 | tf_op jit(solution)/shard_map/ppermute | solution.py:23
  249.6 10.8 %collective-permute-start.7 = (bf16[32,264,4]{1,0,2:T(8,128)(2,1)S(1)}, bf16[32,264,4]{1,0,2:T(8,128)(2,1)S(1)}, u32[]{:S(2)}, u32[]{:S(2)}) collective-permute-start(bf16[32,264,4]{1,0,2:T(8,128)(2,1)S(1)} %copy.40), channel_id=1, source_target_pairs={{0,1},{1,2},{2,3},{3,4},{4,5},{5,6},{6,7},{7,8},{8,9},{9,10},{10,1... | collective-permute-start | bytes 202760 | tf_op jit(solution)/shard_map/ppermute | solution.py:22
  251.5 5.8 collective-permute-start.6
  263.4 7.2 %copy-start.7 = (bf16[32,256,128]{2,0,1:T(8,128)(2,1)S(1)}, bf16[32,256,128]{2,0,1:T(8,128)(2,1)}, u32[]{:S(2)}) copy-start(bf16[32,256,128]{2,0,1:T(8,128)(2,1)} %copy-done.6) | copy-start | bytes 6291460
  263.4 7.2 %copy-start.9 = (bf16[32,256,128]{2,0,1:T(8,128)(2,1)S(1)}, bf16[32,256,128]{2,0,1:T(8,128)(2,1)}, u32[]{:S(2)}) copy-start(bf16[32,256,128]{2,0,1:T(8,128)(2,1)} %multiply_convert_fusion.1) | copy-start | bytes 6291460
  270.7 201.2 %copy-start.10 = (bf16[256,512]{1,0:T(8,128)(2,1)S(1)}, bf16[256,512]{1,0:T(8,128)(2,1)}, u32[]{:S(2)}) copy-start(bf16[256,512]{1,0:T(8,128)(2,1)} %param.7) | copy-start | bytes 786436
  270.7 202.0 %copy-start.11 = (bf16[512,32]{0,1:T(8,128)(2,1)S(1)}, bf16[512,32]{0,1:T(8,128)(2,1)}, u32[]{:S(2)}) copy-start(bf16[512,32]{0,1:T(8,128)(2,1)} %param.8) | copy-start | bytes 98308
  270.7 203.1 %copy-start.12 = (bf16[512,32]{0,1:T(8,128)(2,1)S(1)}, bf16[512,32]{0,1:T(8,128)(2,1)}, u32[]{:S(2)}) copy-start(bf16[512,32]{0,1:T(8,128)(2,1)} %param.9) | copy-start | bytes 98308
  358.2 114.7 %all-to-all-start = ((bf16[32,128,32]{1,2,0:T(8,128)(2,1)}), bf16[32,128,32]{1,2,0:T(8,128)(2,1)S(1)}, u32[]{:S(2)}, u32[]{:S(2)}) async-start(bf16[32,128,32]{1,2,0:T(8,128)(2,1)} %stack.22), calls=%async_computation | async-start | bytes 524288 | tf_op jit(solution)/shard_map/all_to_all | solution.py:126
  366.9 270.7 %all-reduce.4.cloned.1.call-start = ((), (), s32[]{:S(2)}) async-start(), calls=%async_computation.1 | async-start | bytes 262144 | tf_op jit(solution)/shard_map/psum | solution.py:140
Sparse Core Ops, SparseCore 0:
  473.9 163.6 all-reduce.3
